TPU v7x, 32 devices: a whole 2x2x4 slice. The times are simulated.
32 devices in a mesh: leaf: 2 (over core), row: 4 (over y, x), col: 4 (over z).
Axes of the slice: x: 2, y: 2, z: 4, core: 2. Of those that a mesh axis runs over, the one named last changes fastest.
Arguments:
- sketch_leaf: bfloat16 [16384, 256], P(('leaf', 'row'), 'col'), may hold values from -6 to 6
- sketch_sep: bfloat16 [8192, 256], P(('row', 'col')), may hold values from -6 to 6
- leaf_inverse: bfloat16 [16384, 8192], P(('leaf', 'col'), 'row'), as said below
- coupling: bfloat16 [16384, 2048], P(('leaf', 'col'), 'row'), may hold values from -0.0625 to 0.0625
- sep_inverse: bfloat16 [8192, 8192], P('leaf', ('row', 'col'))
- front_map: int32 [2, 16], replicated, may hold values from 0 to 63, as said below
Outputs:
- sketch_out_leaf: float32 [16384, 256], P(('leaf', 'row'), 'col')
- sketch_out_sep: float32 [8192, 256], P(('row', 'col'))
Inputs may be any that keep to these rules, and one draw needn't show every extreme that they name: `front_map`: row block q of every section's coupling lies in separator blocks q * 4 to q * 4 + 3. leaf_inverse and sep_inverse are inverses of lower triangular factor blocks (in natural order), stored in block-cyclic order.
All inputs are finite; a program needn't handle non-finite values.
Results may differ from a plain program's by a relative error of at most 0.024.
Values may be sent and summed in bfloat16 or wider, within the bound.
No kernel may reach another device: no remote copies, remote signals or barrier semaphores. Data moves between devices by JAX's collectives and lax.ppermute only.
A program may use at most 64 MiB of HBM per device.

v0:
```python
import jax
import jax.numpy as jnp
from jax import lax
from jax.sharding import PartitionSpec as P


def contract_rows(left, right):
    return lax.dot_general(
        left, right, (((0,), (0,)), ((), ())), preferred_element_type=jnp.float32
    )


def shards(sketch_leaf, sketch_sep, leaf_inverse, coupling, sep_inverse, front_map):
    columns = sketch_leaf.shape[1] * lax.axis_size("col")
    q_index = lax.axis_index("row") * lax.axis_size("col") + lax.axis_index("col")
    section = lax.axis_index("leaf")
    partial_value = jnp.dot(
        leaf_inverse,
        lax.all_gather(sketch_leaf, "col", axis=1, tiled=True),
        preferred_element_type=jnp.float32,
    )
    front_z = lax.psum_scatter(partial_value, "row", scatter_dimension=1, tiled=True).astype(
        jnp.bfloat16
    )
    coupled_part = contract_rows(coupling, lax.all_gather(front_z, "row", axis=1, tiled=True))
    coupled = lax.psum_scatter(coupled_part, "col", scatter_dimension=0, tiled=True).astype(
        jnp.bfloat16
    )
    block_rows = coupled.shape[0]
    group = sketch_sep.shape[0] // block_rows
    own_slot = front_map[section, q_index] - q_index * group
    blocks = lax.all_gather(coupled, "leaf", axis=0, tiled=True)
    slots = front_map[:, q_index] - q_index * group
    place = (slots[:, None] == jnp.arange(group, dtype=jnp.int32)[None, :]).astype(jnp.bfloat16)
    stacked = blocks.reshape(slots.shape[0], block_rows, columns)
    total = jnp.einsum("sg,sik->gik", place, stacked, preferred_element_type=jnp.float32).reshape(
        group * block_rows, columns
    )
    sep_rhs = (sketch_sep.astype(jnp.float32) - total).astype(jnp.bfloat16)
    sep_part = jnp.dot(sep_inverse, sep_rhs, preferred_element_type=jnp.float32)
    sep_mid = lax.psum(sep_part.astype(jnp.bfloat16), ("row", "col"))
    sketch_out_sep = lax.psum(
        contract_rows(sep_inverse, sep_mid).astype(jnp.bfloat16), "leaf"
    ).astype(jnp.float32)
    sep_round = sketch_out_sep.astype(jnp.bfloat16)
    pulled = lax.dynamic_slice_in_dim(sep_round, own_slot * block_rows, block_rows, 0)
    back_part = jnp.dot(
        coupling,
        lax.all_gather(pulled, "col", axis=0, tiled=True),
        preferred_element_type=jnp.float32,
    )
    back_slice = lax.psum_scatter(
        back_part.astype(jnp.bfloat16), "row", scatter_dimension=1, tiled=True
    ).astype(jnp.float32)
    leaf_rhs = (front_z.astype(jnp.float32) - back_slice).astype(jnp.bfloat16)
    out_part = contract_rows(leaf_inverse, lax.all_gather(leaf_rhs, "row", axis=1, tiled=True))
    sketch_out_leaf = lax.psum_scatter(
        out_part.astype(jnp.bfloat16), "col", scatter_dimension=1, tiled=True
    ).astype(jnp.float32)
    return (sketch_out_leaf, sketch_out_sep)


def solution(mesh):
    placed = (
        P(("leaf", "row"), "col"),
        P(("row", "col"), None),
        P(("leaf", "col"), "row"),
        P(("leaf", "col"), "row"),
        P("leaf", ("row", "col")),
        P(),
    )
    return jax.shard_map(
        shards,
        mesh=mesh,
        in_specs=placed,
        out_specs=(P(("leaf", "row"), "col"), P(("row", "col"), None)),
        check_vma=False,
    )
```

profile of v0, /device:TPU:0, one launch (start us, length us, event | category | flops | bytes accessed | tf_op | source)
XLA Modules:
  0.0 407.7 jit_solution(16510389504449765819)
XLA Ops:
  7.2 0.7 all-gather.4.cloned.1.call-update
  8.0 32.3 %all-gather.4.cloned.1.call-done = bf16[2048,256]{0,1:T(8,128)(2,1)} async-done(((bf16[2048,64]{0,1:T(8,128)(2,1)}), bf16[2048,256]{0,1:T(8,128)(2,1)}) %all-gather.4.cloned.1.call-update) | async-done | bytes 1048592 | tf_op jit(solution)/shard_map/all_gather | solution.py:19
  40.3 7.3 %fusion.10 = f32[2048,256]{0,1:T(8,128)} fusion(bf16[2048,2048]{1,0:T(8,128)(2,1)} %param.8, bf16[2048,256]{0,1:T(8,128)(2,1)} %all-gather.4.cloned.1.call-done), kind=kOutput, calls=%fused_computation.19 | convolution fusion | flops 2147483648 | bytes 11534336 | tf_op jit(solution)/shard_map/dot_general | solution.py:17
  47.7 34.7 %reduce-scatter.5.cloned.1.call-done = f32[2048,64]{0,1:T(8,128)} async-done(((f32[2048,256]{0,1:T(8,128)}), f32[2048,64]{0,1:T(8,128)}) %reduce-scatter.5.cloned.1.call-update) | async-done | bytes 524304 | tf_op jit(solution)/shard_map/reduce_scatter | solution.py:22
  82.3 1.8 convert_element_type.53
  84.2 27.1 %all-gather.6.cloned.1.call-done = bf16[2048,256]{0,1:T(8,128)(2,1)} async-done(((bf16[2048,64]{0,1:T(8,128)(2,1)}), bf16[2048,256]{0,1:T(8,128)(2,1)}) %all-gather.6.cloned.1.call-update) | async-done | bytes 1048592 | tf_op jit(solution)/shard_map/all_gather | solution.py:25
  111.3 2.7 convolution_bitcast_fusion
  114.3 21.7 %reduce-scatter.7.cloned.1.call-done = f32[128,256]{0,1:T(8,128)} async-done(((f32[512,256]{0,1:T(8,128)}), f32[128,256]{0,1:T(8,128)}) %reduce-scatter.7.cloned.1.call-update) | async-done | bytes 131088 | tf_op jit(solution)/shard_map/reduce_scatter | solution.py:26
  136.0 0.9 convert_element_type.56
  136.9 1.9 all_gather.17
  139.7 4.8 %fusion = bf16[4096,256]{0,1:T(8,128)(2,1)} fusion(bf16[512,256]{1,0:T(8,128)(2,1)S(1)} %fusion.4, bf16[4096,512]{1,0:T(8,128)(2,1)} %param.10), kind=kOutput, calls=%fused_computation.1 | convolution fusion | flops 1074790400 | bytes 6553600 | tf_op jit(solution)/shard_map/dot_general | solution.py:40
  144.5 125.0 %all-reduce.3.cloned.1.call-done = bf16[4096,256]{0,1:T(8,128)(2,1)} async-done(((bf16[4096,256]{0,1:T(8,128)(2,1)}), bf16[4096,256]{0,1:T(8,128)(2,1)}) %all-reduce.3.cloned.1.call-update) | async-done | bytes 2097168 | tf_op jit(solution)/shard_map/psum | solution.py:41
  269.5 4.8 %fusion.3 = bf16[512,256]{0,1:T(8,128)(2,1)} fusion(bf16[4096,256]{0,1:T(8,128)(2,1)} %all-reduce.3.cloned.1.call-done, bf16[4096,512]{1,0:T(8,128)(2,1)} %param.10), kind=kOutput, calls=%fused_computation.8 | convolution fusion | flops 1073872896 | bytes 6553600 | tf_op jit(solution)/shard_map/dot_general | solution.py:8
  275.6 16.3 %all-reduce.5.cloned.1.call-done = bf16[512,256]{0,1:T(8,128)(2,1)} async-done(((bf16[512,256]{0,1:T(8,128)(2,1)}), bf16[512,256]{0,1:T(8,128)(2,1)}) %all-reduce.5.cloned.1.call-update) | async-done | bytes 262160 | tf_op jit(solution)/shard_map/psum | solution.py:42
  291.9 0.8 constant_dynamic-slice_fusion
  292.8 13.1 %all_gather.18 = bf16[512,256]{0,1:T(8,128)(2,1)S(1)} all-gather(bf16[128,256]{0,1:T(8,128)(2,1)S(1)} %constant_dynamic-slice_fusion), channel_id=1, replica_groups=mesh['leaf'=2,'row'=4,'col'=4] {'col'}, dimensions={0}, use_global_device_ids=true | all-gather | bytes 327680 | tf_op jit(solution)/shard_map/all_gather | solution.py:49
  305.9 1.7 fusion.2
  307.7 28.2 %reduce-scatter.9.cloned.1.call-done = bf16[2048,64]{0,1:T(8,128)(2,1)} async-done(((bf16[2048,256]{0,1:T(8,128)(2,1)}), bf16[2048,64]{0,1:T(8,128)(2,1)}) %reduce-scatter.9.cloned.1.call-update) | async-done | bytes 262160 | tf_op jit(solution)/shard_map/reduce_scatter | solution.py:52
  335.9 1.7 subtract_convert_fusion
  337.7 27.2 %all-gather.8.cloned.1.call-done = bf16[2048,256]{0,1:T(8,128)(2,1)} async-done(((bf16[2048,64]{0,1:T(8,128)(2,1)}), bf16[2048,256]{0,1:T(8,128)(2,1)}) %all-gather.8.cloned.1.call-update) | async-done | bytes 1048592 | tf_op jit(solution)/shard_map/all_gather | solution.py:56
  364.9 7.0 %fusion.1 = bf16[2048,256]{0,1:T(8,128)(2,1)} fusion(bf16[2048,256]{0,1:T(8,128)(2,1)} %all-gather.8.cloned.1.call-done, bf16[2048,2048]{1,0:T(8,128)(2,1)} %param.8), kind=kOutput, calls=%fused_computation.4 | convolution fusion | flops 2148007936 | bytes 10485760 | tf_op jit(solution)/shard_map/dot_general | solution.py:8
  371.9 0.9 copy.12
  372.9 26.5 %reduce-scatter.11.cloned.1.call-done = bf16[2048,64]{0,1:T(8,128)(2,1)} async-done(((bf16[2048,256]{0,1:T(8,128)(2,1)}), bf16[2048,64]{0,1:T(8,128)(2,1)}) %reduce-scatter.11.cloned.1.call-update) | async-done | bytes 262160 | tf_op jit(solution)/shard_map/reduce_scatter | solution.py:57
  399.4 1.8 convert_element_type.68
  (34 shorter events, 2.1 us)
Async XLA Ops:
  7.2 104.1 %copy-start = (bf16[2048,512]{1,0:T(8,128)(2,1)S(1)}, bf16[2048,512]{1,0:T(8,128)(2,1)}, u32[]{:S(2)}) copy-start(bf16[2048,512]{1,0:T(8,128)(2,1)} %param.9) | copy-start | bytes 6291460
  7.2 33.1 %all-gather.4.cloned.1.call-start = ((), (), s32[]{:S(2)}) async-start(), calls=%async_computation.4 | async-start | bytes 1310720 | tf_op jit(solution)/shard_map/all_gather | solution.py:19
  7.9 74.4 %reduce-scatter.5.cloned.1.call-start = ((), (), s32[]{:S(2)}) async-start(), calls=%async_computation.5 | async-start | bytes 2621440 | tf_op jit(solution)/shard_map/reduce_scatter | solution.py:22
  47.6 63.7 %all-gather.6.cloned.1.call-start = ((), (), s32[]{:S(2)}) async-start(), calls=%async_computation.6 | async-start | bytes 1310720 | tf_op jit(solution)/shard_map/all_gather | solution.py:25
  84.1 30.0 %copy-start.4 = (s32[2,16]{1,0:T(2,128)S(1)}, s32[2,16]{1,0:T(2,128)}, u32[]{:S(2)}) copy-start(s32[2,16]{1,0:T(2,128)} %param.11) | copy-start | bytes 388
  84.2 51.9 %reduce-scatter.7.cloned.1.call-start = ((), (), s32[]{:S(2)}) async-start(), calls=%async_computation.7 | async-start | bytes 655360 | tf_op jit(solution)/shard_map/reduce_scatter | solution.py:26
  114.0 25.5 %copy-start.3 = (bf16[512,256]{1,0:T(8,128)(2,1)S(1)}, bf16[512,256]{1,0:T(8,128)(2,1)}, u32[]{:S(2)}) copy-start(bf16[512,256]{1,0:T(8,128)(2,1)} %param.7) | copy-start | bytes 786436
  114.1 155.5 %all-reduce.3.cloned.1.call-start = ((), (), s32[]{:S(2)}) async-start(), calls=%async_computation.8 | async-start | bytes 4194304 | tf_op jit(solution)/shard_map/psum | solution.py:41
  144.5 147.4 %all-reduce.5.cloned.1.call-start = ((), (), s32[]{:S(2)}) async-start(), calls=%async_computation.9 | async-start | bytes 524288 | tf_op jit(solution)/shard_map/psum | solution.py:42
  274.3 61.6 %reduce-scatter.9.cloned.1.call-start = ((), (), s32[]{:S(2)}) async-start(), calls=%async_computation.10 | async-start | bytes 1310720 | tf_op jit(solution)/shard_map/reduce_scatter | solution.py:52
  305.9 30.0 %copy-start.1 = (f32[2048,64]{0,1:T(8,128)S(1)}, f32[2048,64]{0,1:T(8,128)}, u32[]{:S(2)}) copy-start(f32[2048,64]{0,1:T(8,128)} %reduce-scatter.5.cloned.1.call-done) | copy-start | bytes 1572868
  307.7 57.2 %all-gather.8.cloned.1.call-start = ((), (), s32[]{:S(2)}) async-start(), calls=%async_computation.11 | async-start | bytes 1310720 | tf_op jit(solution)/shard_map/all_gather | solution.py:56
  337.6 34.3 %copy-start.2 = (bf16[512,256]{0,1:T(8,128)(2,1)S(1)}, bf16[512,256]{0,1:T(8,128)(2,1)}, u32[]{:S(2)}) copy-start(bf16[512,256]{0,1:T(8,128)(2,1)} %all-reduce.5.cloned.1.call-done) | copy-start | bytes 786436
  337.7 61.7 %reduce-scatter.11.cloned.1.call-start = ((), (), s32[]{:S(2)}) async-start(), calls=%async_computation.12 | async-start | bytes 1310720 | tf_op jit(solution)/shard_map/reduce_scatter | solution.py:57
Sparse Core Ops, SparseCore 0:
  9.6 30.6 all-gather.3
  47.7 34.5 reduce-scatter.4
  84.8 26.4 all-gather.5
  114.2 21.8 reduce-scatter.6
  144.6 124.8 all-reduce.2
  274.4 17.4 all-reduce.4
  307.8 28.0 reduce-scatter.8
  338.3 26.4 all-gather.7
  372.0 27.2 reduce-scatter.10
where the time goes:
time: 408 us
  waiting for transfers between devices  340 us (83%)
  matrix products  28.8 us (7%)
  blocking collectives  15.1 us (4%)
  between operations  14.6 us (4%)
  other arithmetic  6.41 us (2%)
    psum x1, waiting for transfers between devices, shards(): sep_mid = lax.psum(sep_part.astype(jnp.bfloat16), ('row', 'col'))  125 us
    reduce_scatter x1, waiting for transfers between devices, shards(): lax.psum_scatter(partial_value, 'row', scatter_dimension=1, tiled=True)  34.7 us
    all_gather x1, waiting for transfers between devices, shards(): lax.all_gather(sketch_leaf, 'col', axis=1, tiled=True)  32.3 us
    reduce_scatter x1, waiting for transfers between devices, shards(): lax.psum_scatter(back_part.astype(jnp.bfloat16), 'row', scatter_dimension...  28.2 us
    all_gather x1, waiting for transfers between devices, shards(): lax.all_gather(leaf_rhs, 'row', axis=1, tiled=True)  27.2 us
    all_gather x1, waiting for transfers between devices, shards(): lax.all_gather(front_z, 'row', axis=1, tiled=True)  27.1 us
    reduce_scatter x1, waiting for transfers between devices, shards(): lax.psum_scatter(out_part.astype(jnp.bfloat16), 'col', scatter_dimension=...  26.5 us
    reduce_scatter x1, waiting for transfers between devices, shards(): lax.psum_scatter(coupled_part, 'col', scatter_dimension=0, tiled=True)  21.7 us
  transfers between devices with their start and end apart: 9, of which 9 were waited for; matrix products, arithmetic and copies ran while one was open for 0% of the time, Pallas kernels for 0%

commit v1 on v0

--- a/solution.py
+++ b/solution.py
@@ -2,6 +2,27 @@
 import jax.numpy as jnp
 from jax import lax
 from jax.sharding import PartitionSpec as P
+
+
+def ring_gather(value, axis, dim):
+    devices, place, span = (lax.axis_size(axis), lax.axis_index(axis), value.shape[dim])
+    right = [(i, (i + 1) % devices) for i in range(devices)]
+    downward = [(i, (i - 1) % devices) for i in range(devices)]
+    out = jnp.zeros((*value.shape[:dim], devices * span, *value.shape[dim + 1 :]), value.dtype)
+    out = lax.dynamic_update_slice_in_dim(out, value, place * span, axis=dim)
+    from_left = from_right = value
+    half = devices // 2
+    for step in range(1, half + 1):
+        from_left = lax.ppermute(from_left, axis, right)
+        out = lax.dynamic_update_slice_in_dim(
+            out, from_left, (place - step) % devices * span, axis=dim
+        )
+        if step < devices - half:
+            from_right = lax.ppermute(from_right, axis, downward)
+            out = lax.dynamic_update_slice_in_dim(
+                out, from_right, (place + step) % devices * span, axis=dim
+            )
+    return out
 
 
 def contract_rows(left, right):
@@ -15,9 +36,7 @@
     q_index = lax.axis_index("row") * lax.axis_size("col") + lax.axis_index("col")
     section = lax.axis_index("leaf")
     partial_value = jnp.dot(
-        leaf_inverse,
-        lax.all_gather(sketch_leaf, "col", axis=1, tiled=True),
-        preferred_element_type=jnp.float32,
+        leaf_inverse, ring_gather(sketch_leaf, "col", 1), preferred_element_type=jnp.float32
     )
     front_z = lax.psum_scatter(partial_value, "row", scatter_dimension=1, tiled=True).astype(
         jnp.bfloat16

time: 408 us -> 398 us (0.975)
  waiting for transfers between devices: 340 us -> 322 us
  starting transfers between devices: 0.37 us -> 5.53 us
    all_gather x1 -> x0, waiting for transfers between devices: 32.3 us -> none  [shards(): lax.all_gather(sketch_leaf, 'col', axis=1, tiled=True)]
    ppermute x0 -> x3, waiting for transfers between devices: none -> 15.6 us  [the longest x2 11.1 us: ring_gather(): from_left = lax.ppermute(from_left, axis, right)]
    ppermute x0 -> x3, starting transfers between devices: none -> 5.2 us  [the longest x2 3.11 us: ring_gather(): from_left = lax.ppermute(from_left, axis, right)]
  transfers between devices with their start and end apart: 9 -> 11, of which waited for: 9 -> 11; matrix products, arithmetic and copies ran while one was open for 0% -> 1% of each run, Pallas kernels for 0% -> 0%
where the time goes in v1:
time: 398 us
  waiting for transfers between devices  322 us (81%)
  matrix products  28.5 us (7%)
  blocking collectives  15.1 us (4%)
  between operations  15 us (4%)
  other arithmetic  6.41 us (2%)
  starting transfers between devices  5.53 us (1%)
  local copies, waits for them, and re-layouts  4.76 us (1%)
    psum x1, waiting for transfers between devices, shards(): sep_mid = lax.psum(sep_part.astype(jnp.bfloat16), ('row', 'col'))  125 us
    reduce_scatter x1, waiting for transfers between devices, shards(): lax.psum_scatter(partial_value, 'row', scatter_dimension=1, tiled=True)  34.7 us
    reduce_scatter x1, waiting for transfers between devices, shards(): lax.psum_scatter(back_part.astype(jnp.bfloat16), 'row', scatter_dimension...  28.2 us
    all_gather x1, waiting for transfers between devices, shards(): lax.all_gather(leaf_rhs, 'row', axis=1, tiled=True)  27.2 us
    all_gather x1, waiting for transfers between devices, shards(): lax.all_gather(front_z, 'row', axis=1, tiled=True)  27.1 us
    reduce_scatter x1, waiting for transfers between devices, shards(): lax.psum_scatter(out_part.astype(jnp.bfloat16), 'col', scatter_dimension=...  26.5 us
    reduce_scatter x1, waiting for transfers between devices, shards(): lax.psum_scatter(coupled_part, 'col', scatter_dimension=0, tiled=True)  21.7 us
    psum x1, waiting for transfers between devices, shards(): lax.psum(contract_rows(sep_inverse, sep_mid).astype(jnp.bfloat16), 'leaf')  16.3 us
  transfers between devices with their start and end apart: 11, of which 11 were waited for; matrix products, arithmetic and copies ran while one was open for 1% of the time, Pallas kernels for 0%

profile of v1, /device:TPU:0, one launch (start us, length us, event | category | flops | bytes accessed | tf_op | source)
XLA Modules:
  0.0 397.6 jit_solution(13191104217784781177)
XLA Ops:
  7.2 3.1 collective-permute-start
  10.3 2.1 collective-permute-start.1
  13.6 6.2 %collective-permute-done = bf16[2048,64]{0,1:T(8,128)(2,1)S(1)} collective-permute-done((bf16[2048,64]{0,1:T(8,128)(2,1)}, bf16[2048,64]{0,1:T(8,128)(2,1)S(1)}, u32[]{:S(2)}, u32[]{:S(2)}) %collective-permute-start) | collective-permute-done | bytes 262176 | tf_op jit(solution)/shard_map/ppermute | solution.py:16
  19.8 4.5 %collective-permute-done.1 = bf16[2048,64]{0,1:T(8,128)(2,1)} collective-permute-done((bf16[2048,64]{0,1:T(8,128)(2,1)}, bf16[2048,64]{0,1:T(8,128)(2,1)}, u32[]{:S(2)}, u32[]{:S(2)}) %collective-permute-start.1) | collective-permute-done | bytes 262176 | tf_op jit(solution)/shard_map/ppermute | solution.py:21
  25.2 4.9 %collective-permute-done.2 = bf16[2048,64]{0,1:T(8,128)(2,1)S(1)} collective-permute-done((bf16[2048,64]{0,1:T(8,128)(2,1)S(1)}, bf16[2048,64]{0,1:T(8,128)(2,1)S(1)}, u32[]{:S(2)}, u32[]{:S(2)}) %collective-permute-start.2) | collective-permute-done | bytes 262176 | tf_op jit(solution)/shard_map/ppermute | solution.py:16
  30.2 7.1 %convolution_bitcast_fusion = f32[2048,256]{0,1:T(8,128)} fusion(bf16[2048,256]{0,1:T(8,128)(2,1)S(1)} %constant_dynamic-update-slice_fusion, bf16[2048,2048]{1,0:T(8,128)(2,1)} %param.8), kind=kOutput, calls=%fused_computation.2 | convolution fusion | flops 2147483648 | bytes 11534336 | tf_op jit(solution)/shard_map/dot_general | solution.py:38
  37.3 34.7 %reduce-scatter.5.cloned.1.call-done = f32[2048,64]{0,1:T(8,128)} async-done(((f32[2048,256]{0,1:T(8,128)}), f32[2048,64]{0,1:T(8,128)}) %reduce-scatter.5.cloned.1.call-update) | async-done | bytes 524304 | tf_op jit(solution)/shard_map/reduce_scatter | solution.py:41
  72.0 1.8 convert_element_type.53
  73.9 27.1 %all-gather.3.cloned.1.call-done = bf16[2048,256]{0,1:T(8,128)(2,1)} async-done(((bf16[2048,64]{0,1:T(8,128)(2,1)}), bf16[2048,256]{0,1:T(8,128)(2,1)}) %all-gather.3.cloned.1.call-update) | async-done | bytes 1048592 | tf_op jit(solution)/shard_map/all_gather | solution.py:44
  100.9 2.7 convolution_bitcast_fusion.1
  103.9 21.7 %reduce-scatter.7.cloned.1.call-done = f32[128,256]{0,1:T(8,128)} async-done(((f32[512,256]{0,1:T(8,128)}), f32[128,256]{0,1:T(8,128)}) %reduce-scatter.7.cloned.1.call-update) | async-done | bytes 131088 | tf_op jit(solution)/shard_map/reduce_scatter | solution.py:45
  126.6 1.9 all_gather.13
  129.3 4.8 %fusion = bf16[4096,256]{0,1:T(8,128)(2,1)} fusion(bf16[512,256]{1,0:T(8,128)(2,1)S(1)} %fusion.4, bf16[4096,512]{1,0:T(8,128)(2,1)} %param.10), kind=kOutput, calls=%fused_computation.1 | convolution fusion | flops 1074790400 | bytes 6553600 | tf_op jit(solution)/shard_map/dot_general | solution.py:59
  134.2 125.0 %all-reduce.3.cloned.1.call-done = bf16[4096,256]{0,1:T(8,128)(2,1)} async-done(((bf16[4096,256]{0,1:T(8,128)(2,1)}), bf16[4096,256]{0,1:T(8,128)(2,1)}) %all-reduce.3.cloned.1.call-update) | async-done | bytes 2097168 | tf_op jit(solution)/shard_map/psum | solution.py:60
  259.2 4.8 %fusion.3 = bf16[512,256]{0,1:T(8,128)(2,1)} fusion(bf16[4096,256]{0,1:T(8,128)(2,1)} %all-reduce.3.cloned.1.call-done, bf16[4096,512]{1,0:T(8,128)(2,1)} %param.10), kind=kOutput, calls=%fused_computation.9 | convolution fusion | flops 1073872896 | bytes 6553600 | tf_op jit(solution)/shard_map/dot_general | solution.py:29
  265.3 16.3 %all-reduce.5.cloned.1.call-done = bf16[512,256]{0,1:T(8,128)(2,1)} async-done(((bf16[512,256]{0,1:T(8,128)(2,1)}), bf16[512,256]{0,1:T(8,128)(2,1)}) %all-reduce.5.cloned.1.call-update) | async-done | bytes 262160 | tf_op jit(solution)/shard_map/psum | solution.py:61
  282.4 13.1 %all_gather.14 = bf16[512,256]{0,1:T(8,128)(2,1)S(1)} all-gather(bf16[128,256]{0,1:T(8,128)(2,1)S(1)} %constant_dynamic-slice_fusion), channel_id=1, replica_groups=mesh['leaf'=2,'row'=4,'col'=4] {'col'}, dimensions={0}, use_global_device_ids=true | all-gather | bytes 327680 | tf_op jit(solution)/shard_map/all_gather | solution.py:68
  295.6 1.7 fusion.2
  297.3 28.2 %reduce-scatter.9.cloned.1.call-done = bf16[2048,64]{0,1:T(8,128)(2,1)} async-done(((bf16[2048,256]{0,1:T(8,128)(2,1)}), bf16[2048,64]{0,1:T(8,128)(2,1)}) %reduce-scatter.9.cloned.1.call-update) | async-done | bytes 262160 | tf_op jit(solution)/shard_map/reduce_scatter | solution.py:71
  325.6 1.7 subtract_convert_fusion
  327.3 27.2 %all-gather.5.cloned.1.call-done = bf16[2048,256]{0,1:T(8,128)(2,1)} async-done(((bf16[2048,64]{0,1:T(8,128)(2,1)}), bf16[2048,256]{0,1:T(8,128)(2,1)}) %all-gather.5.cloned.1.call-update) | async-done | bytes 1048592 | tf_op jit(solution)/shard_map/all_gather | solution.py:75
  354.5 7.0 %fusion.1 = bf16[2048,256]{0,1:T(8,128)(2,1)} fusion(bf16[2048,256]{0,1:T(8,128)(2,1)} %all-gather.5.cloned.1.call-done, bf16[2048,2048]{1,0:T(8,128)(2,1)} %param.8), kind=kOutput, calls=%fused_computation.5 | convolution fusion | flops 2148007936 | bytes 10485760 | tf_op jit(solution)/shard_map/dot_general | solution.py:29
  362.5 26.5 %reduce-scatter.11.cloned.1.call-done = bf16[2048,64]{0,1:T(8,128)(2,1)} async-done(((bf16[2048,256]{0,1:T(8,128)(2,1)}), bf16[2048,64]{0,1:T(8,128)(2,1)}) %reduce-scatter.11.cloned.1.call-update) | async-done | bytes 262160 | tf_op jit(solution)/shard_map/reduce_scatter | solution.py:76
  389.0 1.8 convert_element_type.68
  (42 shorter events, 6.8 us)
Async XLA Ops:
  7.2 93.8 %copy-start = (bf16[2048,512]{1,0:T(8,128)(2,1)S(1)}, bf16[2048,512]{1,0:T(8,128)(2,1)}, u32[]{:S(2)}) copy-start(bf16[2048,512]{1,0:T(8,128)(2,1)} %param.9) | copy-start | bytes 6291460
  7.2 64.8 %reduce-scatter.5.cloned.1.call-start = ((), (), s32[]{:S(2)}) async-start(), calls=%async_computation.4 | async-start | bytes 2621440 | tf_op jit(solution)/shard_map/reduce_scatter | solution.py:41
  7.2 12.5 %collective-permute-start = (bf16[2048,64]{0,1:T(8,128)(2,1)}, bf16[2048,64]{0,1:T(8,128)(2,1)S(1)}, u32[]{:S(2)}, u32[]{:S(2)}) collective-permute-start(bf16[2048,64]{0,1:T(8,128)(2,1)} %param.6), channel_id=1, source_target_pairs={{0,1},{1,2},{2,3},{3,0},{4,5},{5,6},{6,7},{7,4},{8,9},{9,10},{10,1... | collective-permute-start | bytes 786440 | tf_op jit(solution)/shard_map/ppermute | solution.py:16
  10.3 13.9 %collective-permute-start.1 = (bf16[2048,64]{0,1:T(8,128)(2,1)}, bf16[2048,64]{0,1:T(8,128)(2,1)}, u32[]{:S(2)}, u32[]{:S(2)}) collective-permute-start(bf16[2048,64]{0,1:T(8,128)(2,1)} %param.6), channel_id=1, source_target_pairs={{0,3},{1,0},{2,1},{3,2},{4,7},{5,4},{6,5},{7,6},{8,11},{9,8},{10,9... | collective-permute-start | bytes 786440 | tf_op jit(solution)/shard_map/ppermute | solution.py:21
  19.8 10.4 %collective-permute-start.2 = (bf16[2048,64]{0,1:T(8,128)(2,1)S(1)}, bf16[2048,64]{0,1:T(8,128)(2,1)S(1)}, u32[]{:S(2)}, u32[]{:S(2)}) collective-permute-start(bf16[2048,64]{0,1:T(8,128)(2,1)S(1)} %collective-permute-done), channel_id=1, source_target_pairs={{0,1},{1,2},{2,3},{3,0},{4,5},{5,6},{6,7},{7,4},{8,9},{9,10},{10,1... | collective-permute-start | bytes 786440 | tf_op jit(solution)/shard_map/ppermute | solution.py:16
  37.3 63.7 %all-gather.3.cloned.1.call-start = ((), (), s32[]{:S(2)}) async-start(), calls=%async_computation.5 | async-start | bytes 1310720 | tf_op jit(solution)/shard_map/all_gather | solution.py:44
  73.8 30.0 %copy-start.4 = (s32[2,16]{1,0:T(2,128)S(1)}, s32[2,16]{1,0:T(2,128)}, u32[]{:S(2)}) copy-start(s32[2,16]{1,0:T(2,128)} %param.11) | copy-start | bytes 388
  73.8 51.9 %reduce-scatter.7.cloned.1.call-start = ((), (), s32[]{:S(2)}) async-start(), calls=%async_computation.6 | async-start | bytes 655360 | tf_op jit(solution)/shard_map/reduce_scatter | solution.py:45
  103.7 25.5 %copy-start.3 = (bf16[512,256]{1,0:T(8,128)(2,1)S(1)}, bf16[512,256]{1,0:T(8,128)(2,1)}, u32[]{:S(2)}) copy-start(bf16[512,256]{1,0:T(8,128)(2,1)} %param.7) | copy-start | bytes 786436
  103.7 155.5 %all-reduce.3.cloned.1.call-start = ((), (), s32[]{:S(2)}) async-start(), calls=%async_computation.7 | async-start | bytes 4194304 | tf_op jit(solution)/shard_map/psum | solution.py:60
  134.1 147.4 %all-reduce.5.cloned.1.call-start = ((), (), s32[]{:S(2)}) async-start(), calls=%async_computation.8 | async-start | bytes 524288 | tf_op jit(solution)/shard_map/psum | solution.py:61
  264.0 61.6 %reduce-scatter.9.cloned.1.call-start = ((), (), s32[]{:S(2)}) async-start(), calls=%async_computation.9 | async-start | bytes 1310720 | tf_op jit(solution)/shard_map/reduce_scatter | solution.py:71
  295.6 30.0 %copy-start.1 = (f32[2048,64]{0,1:T(8,128)S(1)}, f32[2048,64]{0,1:T(8,128)}, u32[]{:S(2)}) copy-start(f32[2048,64]{0,1:T(8,128)} %reduce-scatter.5.cloned.1.call-done) | copy-start | bytes 1572868
  297.3 57.2 %all-gather.5.cloned.1.call-start = ((), (), s32[]{:S(2)}) async-start(), calls=%async_computation.10 | async-start | bytes 1310720 | tf_op jit(solution)/shard_map/all_gather | solution.py:75
  327.3 34.3 %copy-start.2 = (bf16[512,256]{0,1:T(8,128)(2,1)S(1)}, bf16[512,256]{0,1:T(8,128)(2,1)}, u32[]{:S(2)}) copy-start(bf16[512,256]{0,1:T(8,128)(2,1)} %all-reduce.5.cloned.1.call-done) | copy-start | bytes 786436
  327.3 61.7 %reduce-scatter.11.cloned.1.call-start = ((), (), s32[]{:S(2)}) async-start(), calls=%async_computation.11 | async-start | bytes 1310720 | tf_op jit(solution)/shard_map/reduce_scatter | solution.py:76
Sparse Core Ops, SparseCore 0:
  37.4 34.5 reduce-scatter.4
  74.4 26.4 all-gather.2
  103.8 21.8 reduce-scatter.6
  134.3 124.8 all-reduce.2
  264.1 17.4 all-reduce.4
  297.4 28.0 reduce-scatter.8
  328.0 26.4 all-gather.4
  361.7 27.2 reduce-scatter.10
